TPU v7x, 512 devices: a whole 4x4x16 slice. The times are simulated.
512 devices in a mesh: slab: 64 (over z_lo, x, core), grp: 8 (over z_hi, y).
Axes of the slice: x: 4, y: 4, z: 16 (z_hi: 2, z_lo: 8; z = z_hi * 8 + z_lo), core: 2. Of those that a mesh axis runs over, the one named last changes fastest.
Arguments:
- adj_out: float32 [5, 512, 256, 256], P(None, 'grp', 'slab'), may hold values from -6 to 6
- advect: bfloat16 [3, 512, 256, 256], P(None, 'grp', 'slab'), may hold values from -4 to 4
- viscosity: bfloat16 [512, 256, 256], P('grp', 'slab'), may hold values from 0.099609375 to 0.796875
- body_mask: int32 [512, 256, 256], P('grp', 'slab'), may hold values 0 or 1
- marker_x: int32 [2048], replicated, may hold values from 128 to 191
- marker_z: int32 [2048], replicated, may hold values from 0 to 255
- marker_y: int32 [2048], replicated, may hold values from 64 to 191
- drag_weight: float32 [2048], replicated, may hold values from -5 to 5
- inv_x: float32 [512, 512], P(None, 'grp'), may hold values from 0 to 1, as said below
- inv_y: float32 [256, 256], replicated, may hold values from 0 to 1, as said below
- inv_z: float32 [256, 256], replicated, may hold values from 0 to 1, as said below
Outputs:
- state_adjoint: float32 [5, 512, 256, 256], P(None, 'grp', 'slab')
Inputs may be any that keep to these rules, and one draw needn't show every extreme that they name: `inv_x`: entries of a given inverse. `inv_y`: entries of a given inverse. `inv_z`: entries of a given inverse.
All inputs are finite; a program needn't handle non-finite values. No bound on the sum of `body_mask` on one device may be relied on, other than what follows from the above.
Results may differ from a plain program's by a relative error of at most 0.0003.
Values sent between devices are 32-bit elements; how exact they have to be, the bound alone decides.
No kernel may reach another device: no remote copies, remote signals or barrier semaphores. Data moves between devices by JAX's collectives and lax.ppermute only.
A program may use at most 64 MiB of HBM per device.

v0:
```python
import jax
import jax.numpy as jnp
from jax import lax
from jax.sharding import PartitionSpec as P

time_step = 0.08
highest = lax.Precision.HIGHEST


def extended(cells, sides, width):
    for axis, dim in sides:
        count = lax.axis_size(axis)
        ends = count - 1
        head = lax.slice_in_dim(cells, 0, width, axis=dim)
        tail = lax.slice_in_dim(cells, cells.shape[dim] - width, cells.shape[dim], axis=dim)
        cells = jnp.concatenate(
            [
                lax.ppermute(tail, axis, [(i, (i + 1) % count) for i in range(ends)]),
                cells,
                lax.ppermute(head, axis, [((i + 1) % count, i) for i in range(ends)]),
            ],
            axis=dim,
        )
    return cells


def body(
    adj_out,
    advect,
    viscosity,
    body_mask,
    marker_x,
    marker_z,
    marker_y,
    drag_weight,
    inv_x,
    inv_y,
    inv_z,
):
    fields, x_rows, z_rows, y_cells = adj_out.shape
    x_offset = lax.axis_index("grp") * x_rows
    z_offset = lax.axis_index("slab") * z_rows
    local_x = marker_x - x_offset
    local_z = marker_z - z_offset
    inside = (local_x >= 0) & (local_x < x_rows) & (local_z >= 0) & (local_z < z_rows)
    flat_index = jnp.where(inside, (local_x * z_rows + local_z) * y_cells + marker_y, 0)
    pushed = jax.ops.segment_sum(
        jnp.where(inside, drag_weight, 0.0), flat_index, num_segments=x_rows * z_rows * y_cells
    )
    seeded = adj_out.at[0].add(pushed.reshape(x_rows, z_rows, y_cells))
    zlines = lax.all_to_all(seeded, "slab", split_axis=1, concat_axis=2, tiled=True)
    zlines = jnp.einsum("jk,cxjy->cxky", inv_z, zlines, precision=highest)
    zlines = jnp.einsum("jk,cxzj->cxzk", inv_y, zlines, precision=highest)
    returned = lax.all_to_all(zlines, "slab", split_axis=2, concat_axis=1, tiled=True)
    solved = jnp.einsum(
        "jk,cjzy->ckzy",
        inv_x,
        lax.all_gather(returned, "grp", axis=1, tiled=True),
        precision=highest,
    )
    masked = solved * body_mask.astype(jnp.float32)
    rimmed = extended(masked, (("slab", 2), ("grp", 1)), 1)
    centre = rimmed[:, 1:-1, 1:-1, :]
    y_padded = jnp.pad(centre, ((0, 0), (0, 0), (0, 0), (1, 1)))
    grad_x = (rimmed[:, 2:, 1:-1, :] - rimmed[:, :-2, 1:-1, :]) * 0.5
    grad_z = (rimmed[:, 1:-1, 2:, :] - rimmed[:, 1:-1, :-2, :]) * 0.5
    grad_y = (y_padded[..., 2:] - y_padded[..., :-2]) * 0.5
    laplace = (
        rimmed[:, 2:, 1:-1, :]
        + rimmed[:, :-2, 1:-1, :]
        + rimmed[:, 1:-1, 2:, :]
        + rimmed[:, 1:-1, :-2, :]
        + y_padded[..., 2:]
        + y_padded[..., :-2]
        - 6.0 * centre
    )
    velocity = advect.astype(jnp.float32)
    viscous = viscosity.astype(jnp.float32)
    change = velocity[0] * grad_x + velocity[1] * grad_z + velocity[2] * grad_y + viscous * laplace
    return centre + time_step * change


def solution(mesh):
    in_specs = (
        P(None, "grp", "slab", None),
        P(None, "grp", "slab", None),
        P("grp", "slab", None),
        P("grp", "slab", None),
        P(),
        P(),
        P(),
        P(),
        P(None, "grp"),
        P(),
        P(),
    )
    out_specs = P(None, "grp", "slab", None)
    return jax.shard_map(body, mesh=mesh, in_specs=in_specs, out_specs=out_specs, check_vma=False)
```

profile of v0, /device:TPU:352, one launch (start us, length us, event | category | flops | bytes accessed | tf_op | source)
XLA Modules:
  0.0 591.5 jit_solution(2021794597790402186)
XLA Ops:
  6.5 0.0 copy-start
  6.5 0.0 all-gather.2.cloned.1.call-start
  6.5 0.8 add_select_fusion
  7.3 0.7 broadcast_select_fusion
  8.1 14.8 %scatter_custom_fusion = f32[65536]{0:T(1024)S(1)} fusion(s32[2048]{0:T(1024)S(1)} %add_select_fusion, f32[2048]{0:T(1024)S(1)} %broadcast_select_fusion, f32[]{:T(128)} %constant.45.clone.1), kind=kCustom, calls=%fused_computation.27 | custom fusion | flops 2048 | bytes 262148 | tf_op jit(solution)/shard_map/scatter-add | solution.py:47
  22.8 0.1 reshape.62
  23.0 1.5 copy.57
  24.5 0.1 fusion.4
  24.6 68.9 %all_to_all.21 = f32[5,64,4,256]{3,2,0,1:T(4,128)S(1)} all-to-all(f32[5,64,4,256]{3,2,0,1:T(4,128)S(1)} %fusion.4), channel_id=1, replica_groups=mesh['slab'=64,'grp'=8] {'slab'}, dimensions={1} | all-to-all | bytes 2621440 | tf_op jit(solution)/shard_map/all_to_all | solution.py:51
  93.5 0.2 copy.58
  93.8 0.5 reshape.63
  94.2 0.0 copy-done
  94.2 0.0 copy-start.3
  94.3 2.2 convolution_bitcast_fusion.1
  96.5 0.0 copy-done.3
  96.5 2.3 convolution_bitcast_fusion
  98.8 1.3 copy.61
  100.1 70.3 %all_to_all.22 = f32[5,1,256,256]{3,1,0,2:T(1,128)S(1)} all-to-all(f32[5,1,256,256]{3,1,0,2:T(1,128)S(1)} %copy.61), channel_id=1, replica_groups=mesh['slab'=64,'grp'=8] {'slab'}, dimensions={2} | all-to-all | bytes 2621440 | tf_op jit(solution)/shard_map/all_to_all | solution.py:54
  170.4 0.3 copy.75
  170.7 1.8 copy.63
  172.5 0.0 copy-start.2
  172.5 0.0 copy-start.4
  172.5 0.0 all-gather.2.cloned.1.call-update
  172.5 0.9 copy-done.2
  173.5 0.1 copy.64
  173.6 324.0 %all-gather.2.cloned.1.call-done = f32[5,512,4,256]{3,1,2,0:T(8,128)} async-done(((f32[5,64,4,256]{3,1,2,0:T(8,128)}), f32[5,512,4,256]{3,1,2,0:T(8,128)}) %all-gather.2.cloned.1.call-update) | async-done | bytes 10485776 | tf_op jit(solution)/shard_map/all_gather | solution.py:58
  497.6 0.0 copy-done.4
  497.6 9.5 %fusion = f32[5,64,4,256]{3,1,2,0:T(8,128)S(1)} fusion(f32[5,512,4,256]{3,1,2,0:T(8,128)} %all-gather.2.cloned.1.call-done, f32[64,4,256]{2,0,1:T(8,128)S(1)} %copy.64, f32[512,64]{0,1:T(8,128)S(1)} %copy-done.4), kind=kOutput, calls=%fused_computation.6 | convolution fusion | flops 2013593600 | bytes 12189696 | tf_op jit(solution)/shard_map/jk,cjzy->ckzy/dot_general | solution.py:55
  507.1 0.0 copy-start.1
  507.2 0.1 fusion.10
  507.2 2.1 collective-permute-start
  509.3 38.0 %collective-permute-start.1 = (f32[5,64,1,256]{3,1,2,0:T(8,128)S(1)}, f32[5,64,1,256]{3,1,2,0:T(8,128)S(1)}, u32[]{:S(2)}, u32[]{:S(2)}) collective-permute-start(f32[5,64,1,256]{3,1,2,0:T(8,128)S(1)} %get-tuple-element.20), channel_id=1, source_target_pairs={{8,0},{16,8},{24,16},{32,24},{40,32},{48,40},{56,48},{64,56},{72,6... | collective-permute-start | bytes 983048 | tf_op jit(solution)/shard_map/ppermute | solution.py:20
  547.3 0.0 copy-done.1
  547.3 0.1 convert_element_type.12
  547.5 2.7 collective-permute-done
  550.1 2.1 collective-permute-done.1
  552.3 11.7 %collective-permute-start.2 = (f32[5,1,6,256]{3,1,2,0:T(1,128)S(1)}, f32[5,1,6,256]{3,1,2,0:T(1,128)S(1)}, u32[]{:S(2)}, u32[]{:S(2)}) collective-permute-start(f32[5,1,6,256]{3,1,2,0:T(1,128)S(1)} %get-tuple-element.18), channel_id=1, source_target_pairs={{1,0},{2,1},{3,2},{4,3},{5,4},{6,5},{7,6},{9,8},{10,9},{11,10},{12... | collective-permute-start | bytes 92168 | tf_op jit(solution)/shard_map/ppermute | solution.py:20
  564.0 0.0 copy-start.5
  564.0 2.1 collective-permute-start.3
  566.1 0.2 fusion.3
  566.3 0.1 copy.65
  566.3 0.1 copy.66
  566.4 0.1 copy.67
  566.4 0.0 copy-done.5
  566.5 0.0 collective-permute-done.2
  566.5 14.3 %collective-permute-done.3 = f32[5,1,6,256]{3,1,2,0:T(1,128)S(1)} collective-permute-done((f32[5,1,6,256]{3,1,2,0:T(1,128)S(1)}, f32[5,1,6,256]{3,1,2,0:T(1,128)S(1)}, u32[]{:S(2)}, u32[]{:S(2)}) %collective-permute-start.3) | collective-permute-done | bytes 30752 | tf_op jit(solution)/shard_map/ppermute | solution.py:18
  580.7 2.0 multiply_add_fusion
  582.8 1.9 copy.69
  (3 shorter events, 0.1 us)
Async XLA Ops:
  6.5 87.7 %copy-start = (f32[256,256]{1,0:T(8,128)S(1)}, f32[256,256]{1,0:T(8,128)}, u32[]{:S(2)}) copy-start(f32[256,256]{1,0:T(8,128)} %param.23) | copy-start | bytes 786436
  6.5 491.1 %all-gather.2.cloned.1.call-start = ((), (), s32[]{:S(2)}) async-start(), calls=%async_computation.2 | async-start | bytes 11796480 | tf_op jit(solution)/shard_map/all_gather | solution.py:58
  94.2 2.2 copy-start.3
  172.5 0.9 copy-start.2
  172.5 325.1 %copy-start.4 = (f32[512,64]{0,1:T(8,128)S(1)}, f32[512,64]{0,1:T(8,128)}, u32[]{:S(2)}) copy-start(f32[512,64]{0,1:T(8,128)} %param.21) | copy-start | bytes 393220
  507.1 40.2 %copy-start.1 = (bf16[3,64,4,256]{3,2,1,0:T(4,128)(2,1)S(1)}, bf16[3,64,4,256]{3,2,1,0:T(4,128)(2,1)}, u32[]{:S(2)}) copy-start(bf16[3,64,4,256]{3,2,1,0:T(4,128)(2,1)} %param.14) | copy-start | bytes 1179652
  507.2 42.9 %collective-permute-start = (f32[5,64,1,256]{3,1,2,0:T(8,128)S(1)}, f32[5,64,1,256]{3,1,2,0:T(8,128)S(1)}, u32[]{:S(2)}, u32[]{:S(2)}) collective-permute-start(f32[5,64,1,256]{3,1,2,0:T(8,128)S(1)} %get-tuple-element.19), channel_id=1, source_target_pairs={{0,8},{8,16},{16,24},{24,32},{32,40},{40,48},{48,56},{56,64},{64,7... | collective-permute-start | bytes 983048 | tf_op jit(solution)/shard_map/ppermute | solution.py:18
  509.3 42.9 %collective-permute-start.1 = (f32[5,64,1,256]{3,1,2,0:T(8,128)S(1)}, f32[5,64,1,256]{3,1,2,0:T(8,128)S(1)}, u32[]{:S(2)}, u32[]{:S(2)}) collective-permute-start(f32[5,64,1,256]{3,1,2,0:T(8,128)S(1)} %get-tuple-element.20), channel_id=1, source_target_pairs={{8,0},{16,8},{24,16},{32,24},{40,32},{48,40},{56,48},{64,56},{72,6... | collective-permute-start | bytes 983048 | tf_op jit(solution)/shard_map/ppermute | solution.py:20
  552.3 14.2 %collective-permute-start.2 = (f32[5,1,6,256]{3,1,2,0:T(1,128)S(1)}, f32[5,1,6,256]{3,1,2,0:T(1,128)S(1)}, u32[]{:S(2)}, u32[]{:S(2)}) collective-permute-start(f32[5,1,6,256]{3,1,2,0:T(1,128)S(1)} %get-tuple-element.18), channel_id=1, source_target_pairs={{1,0},{2,1},{3,2},{4,3},{5,4},{6,5},{7,6},{9,8},{10,9},{11,10},{12... | collective-permute-start | bytes 92168 | tf_op jit(solution)/shard_map/ppermute | solution.py:20
  564.0 2.5 copy-start.5
  564.0 16.7 %collective-permute-start.3 = (f32[5,1,6,256]{3,1,2,0:T(1,128)S(1)}, f32[5,1,6,256]{3,1,2,0:T(1,128)S(1)}, u32[]{:S(2)}, u32[]{:S(2)}) collective-permute-start(f32[5,1,6,256]{3,1,2,0:T(1,128)S(1)} %get-tuple-element.17), channel_id=1, source_target_pairs={{0,1},{1,2},{2,3},{3,4},{4,5},{5,6},{6,7},{8,9},{9,10},{10,11},{11... | collective-permute-start | bytes 92168 | tf_op jit(solution)/shard_map/ppermute | solution.py:18
Sparse Core Ops, SparseCore 0:
  172.7 324.8 all-gather.1
where the time goes:
time: 592 us
  waiting for transfers between devices  343 us (58%)
  blocking collectives  139 us (23%)
  starting transfers between devices  53.8 us (9%)
  other arithmetic  18.8 us (3%)
  matrix products  14 us (2%)
  between operations  13.6 us (2%)
  local copies, waits for them, and re-layouts  8.92 us (2%)
    all_gather x1, waiting for transfers between devices, body(): lax.all_gather(returned, 'grp', axis=1, tiled=True)  324 us
    all_to_all x1, blocking collectives, body(): lax.all_to_all(zlines, 'slab', split_axis=2, concat_axis=1, tiled=True)  70.3 us
    all_to_all x1, blocking collectives, body(): lax.all_to_all(seeded, 'slab', split_axis=1, concat_axis=2, tiled=True)  68.9 us
    ppermute x2, starting transfers between devices, extended(): lax.ppermute(head, axis, [((i + 1) % count, i) for i in range(ends)])  49.7 us
    ppermute x2, waiting for transfers between devices, extended(): lax.ppermute(tail, axis, [(i, (i + 1) % count) for i in range(ends)])  17 us
    scatter-add x1, other arithmetic, body(): jax.ops.segment_sum(jnp.where(inside, drag_weight, 0.0), flat_index, num_...  14.8 us
  transfers between devices with their start and end apart: 5, of which 4 were waited for; matrix products, arithmetic and copies ran while one was open for 0% of the time, Pallas kernels for 0%

commit v1 on v0

--- a/solution.py
+++ b/solution.py
@@ -5,6 +5,13 @@
 
 time_step = 0.08
 highest = lax.Precision.HIGHEST
+
+
+def all_by_exchange(array, name, along):
+    count = lax.axis_size(name)
+    blocks = jnp.stack([array for _ in range(count)])
+    blocks = lax.all_to_all(blocks, name, split_axis=0, concat_axis=0)
+    return jnp.concatenate(blocks, axis=along)
 
 
 def extended(cells, sides, width):
@@ -53,10 +60,7 @@
     zlines = jnp.einsum("jk,cxzj->cxzk", inv_y, zlines, precision=highest)
     returned = lax.all_to_all(zlines, "slab", split_axis=2, concat_axis=1, tiled=True)
     solved = jnp.einsum(
-        "jk,cjzy->ckzy",
-        inv_x,
-        lax.all_gather(returned, "grp", axis=1, tiled=True),
-        precision=highest,
+        "jk,cjzy->ckzy", inv_x, all_by_exchange(returned, "grp", 1), precision=highest
     )
     masked = solved * body_mask.astype(jnp.float32)
     rimmed = extended(masked, (("slab", 2), ("grp", 1)), 1)

time: 592 us -> 749 us (1.27)
  the two profiles are of different devices: /device:TPU:352 before, /device:TPU:451 now
where the time goes in v1:
time: 749 us; the launch traced here: 748 us
  waiting for transfers between devices  385 us (51%)
  starting transfers between devices  179 us (24%)
  blocking collectives  136 us (18%)
  other arithmetic  18.8 us (3%)
  local copies, waits for them, and re-layouts  17 us (2%)
  matrix products  11.5 us (2%)
    all_to_all x1, waiting for transfers between devices, all_by_exchange(): blocks = lax.all_to_all(blocks, name, split_axis=0, concat_axis=0)  367 us
    ppermute x2, starting transfers between devices, extended(): lax.ppermute(tail, axis, [(i, (i + 1) % count) for i in range(ends)])  161 us
    all_to_all x1, blocking collectives, body(): lax.all_to_all(zlines, 'slab', split_axis=2, concat_axis=1, tiled=True)  70.3 us
    all_to_all x1, blocking collectives, body(): lax.all_to_all(seeded, 'slab', split_axis=1, concat_axis=2, tiled=True)  66.2 us
  transfers between devices with their start and end apart: 5, of which 4 were waited for; matrix products, arithmetic and copies ran while one was open for 0% of the time, Pallas kernels for 0%

profile of v1, /device:TPU:451, one launch (start us, length us, event | category | flops | bytes accessed | tf_op | source)
XLA Modules:
  0.0 748.1 jit_solution(1596121770959227905)
XLA Ops:
  0.0 0.0 copy-start
  0.0 0.8 add_select_fusion
  0.8 0.7 broadcast_select_fusion
  1.5 14.8 %scatter_custom_fusion = f32[65536]{0:T(1024)S(1)} fusion(s32[2048]{0:T(1024)S(1)} %add_select_fusion, f32[2048]{0:T(1024)S(1)} %broadcast_select_fusion, f32[]{:T(128)} %constant.45.clone.1), kind=kCustom, calls=%fused_computation.27 | custom fusion | flops 2048 | bytes 262148 | tf_op jit(solution)/shard_map/scatter-add | solution.py:54
  16.3 0.1 reshape.71
  16.4 1.5 copy.59
  18.0 0.1 fusion.4
  18.1 66.2 %all_to_all.23 = f32[5,64,4,256]{3,2,0,1:T(4,128)S(1)} all-to-all(f32[5,64,4,256]{3,2,0,1:T(4,128)S(1)} %fusion.4), channel_id=1, replica_groups=mesh['slab'=64,'grp'=8] {'slab'}, dimensions={1} | all-to-all | bytes 2621440 | tf_op jit(solution)/shard_map/all_to_all | solution.py:58
  84.3 0.2 copy.60
  84.5 0.5 reshape.72
  84.9 0.0 copy-done
  84.9 0.0 copy-start.3
  85.0 2.2 convolution_bitcast_fusion.1
  87.2 0.0 copy-done.3
  87.2 2.3 convolution_bitcast_fusion
  89.5 1.3 copy.63
  90.8 70.3 %all_to_all.24 = f32[5,1,256,256]{3,1,0,2:T(1,128)S(1)} all-to-all(f32[5,1,256,256]{3,1,0,2:T(1,128)S(1)} %copy.63), channel_id=1, replica_groups=mesh['slab'=64,'grp'=8] {'slab'}, dimensions={2} | all-to-all | bytes 2621440 | tf_op jit(solution)/shard_map/all_to_all | solution.py:61
  161.1 0.3 copy.78
  161.4 0.8 copy.65
  162.2 5.1 stack.5
  167.3 0.0 copy-start.2
  167.3 14.2 %all-to-all-start.2 = ((f32[8,5,64,4,256]{4,2,3,1,0:T(8,128)}), f32[8,5,64,4,256]{4,2,3,1,0:T(8,128)}, u32[]{:S(2)}, u32[]{:S(2)}) async-start(f32[8,5,64,4,256]{4,2,3,1,0:T(8,128)} %stack.5), calls=%async_computation.2 | async-start | bytes 20971520 | tf_op jit(solution)/shard_map/all_to_all | solution.py:13
  181.5 0.0 copy-done.2
  181.6 0.1 copy.67
  181.6 366.7 %all-to-all-done.2 = f32[8,5,64,4,256]{4,2,3,1,0:T(8,128)} async-done(((f32[8,5,64,4,256]{4,2,3,1,0:T(8,128)}), f32[8,5,64,4,256]{4,2,3,1,0:T(8,128)}, u32[]{:S(2)}, u32[]{:S(2)}) %all-to-all-start.2) | async-done | bytes 10485792 | tf_op jit(solution)/shard_map/all_to_all | solution.py:13
  548.4 0.0 copy-start.4
  548.4 4.9 copy.66
  553.2 0.0 copy-done.4
  553.2 7.0 fusion
  560.3 0.1 fusion.10
  560.3 157.6 %collective-permute-start = (f32[5,64,1,256]{3,1,2,0:T(8,128)S(1)}, f32[5,64,1,256]{3,1,2,0:T(8,128)S(1)}, u32[]{:S(2)}, u32[]{:S(2)}) collective-permute-start(f32[5,64,1,256]{3,1,2,0:T(8,128)S(1)} %get-tuple-element.19), channel_id=1, source_target_pairs={{0,8},{8,16},{16,24},{24,32},{32,40},{40,48},{48,56},{56,64},{64,7... | collective-permute-start | bytes 983048 | tf_op jit(solution)/shard_map/ppermute | solution.py:25
  717.9 1.9 collective-permute-start.1
  719.8 0.0 copy-done.1
  719.9 0.1 convert_element_type.12
  720.0 1.9 collective-permute-done
  721.9 4.7 collective-permute-done.1
  726.7 1.9 collective-permute-start.2
  728.6 0.0 copy-start.5
  728.6 3.5 collective-permute-start.3
  732.1 0.2 fusion.3
  732.3 0.1 copy.68
  732.4 0.1 copy.69
  732.4 0.1 copy.70
  732.5 0.0 copy-done.5
  732.5 0.0 collective-permute-done.2
  732.5 11.7 %collective-permute-done.3 = f32[5,1,6,256]{3,1,2,0:T(1,128)S(1)} collective-permute-done((f32[5,1,6,256]{3,1,2,0:T(1,128)S(1)}, f32[5,1,6,256]{3,1,2,0:T(1,128)S(1)}, u32[]{:S(2)}, u32[]{:S(2)}) %collective-permute-start.3) | collective-permute-done | bytes 30752 | tf_op jit(solution)/shard_map/ppermute | solution.py:25
  744.2 2.0 multiply_add_fusion
  746.2 1.9 copy.72
  (4 shorter events, 0.1 us)
Async XLA Ops:
  0.0 84.9 %copy-start = (f32[256,256]{1,0:T(8,128)S(1)}, f32[256,256]{1,0:T(8,128)}, u32[]{:S(2)}) copy-start(f32[256,256]{1,0:T(8,128)} %param.23) | copy-start | bytes 786436
  84.9 2.2 copy-start.3
  167.3 14.2 %copy-start.2 = (s32[64,4,256]{2,1,0:T(4,128)S(1)}, s32[64,4,256]{2,1,0:T(4,128)}, u32[]{:S(2)}) copy-start(s32[64,4,256]{2,1,0:T(4,128)} %param.16) | copy-start | bytes 786436
  167.3 381.0 %all-to-all-start.2 = ((f32[8,5,64,4,256]{4,2,3,1,0:T(8,128)}), f32[8,5,64,4,256]{4,2,3,1,0:T(8,128)}, u32[]{:S(2)}, u32[]{:S(2)}) async-start(f32[8,5,64,4,256]{4,2,3,1,0:T(8,128)} %stack.5), calls=%async_computation.2 | async-start | bytes 20971520 | tf_op jit(solution)/shard_map/all_to_all | solution.py:13
  548.4 4.9 copy-start.4
  560.3 159.6 %copy-start.1 = (bf16[3,64,4,256]{3,2,1,0:T(4,128)(2,1)S(1)}, bf16[3,64,4,256]{3,2,1,0:T(4,128)(2,1)}, u32[]{:S(2)}) copy-start(bf16[3,64,4,256]{3,2,1,0:T(4,128)(2,1)} %param.14) | copy-start | bytes 1179652
  560.3 161.6 %collective-permute-start = (f32[5,64,1,256]{3,1,2,0:T(8,128)S(1)}, f32[5,64,1,256]{3,1,2,0:T(8,128)S(1)}, u32[]{:S(2)}, u32[]{:S(2)}) collective-permute-start(f32[5,64,1,256]{3,1,2,0:T(8,128)S(1)} %get-tuple-element.19), channel_id=1, source_target_pairs={{0,8},{8,16},{16,24},{24,32},{32,40},{40,48},{48,56},{56,64},{64,7... | collective-permute-start | bytes 983048 | tf_op jit(solution)/shard_map/ppermute | solution.py:25
  717.9 8.7 %collective-permute-start.1 = (f32[5,64,1,256]{3,1,2,0:T(8,128)S(1)}, f32[5,64,1,256]{3,1,2,0:T(8,128)S(1)}, u32[]{:S(2)}, u32[]{:S(2)}) collective-permute-start(f32[5,64,1,256]{3,1,2,0:T(8,128)S(1)} %get-tuple-element.20), channel_id=1, source_target_pairs={{8,0},{16,8},{24,16},{32,24},{40,32},{48,40},{56,48},{64,56},{72,6... | collective-permute-start | bytes 983048 | tf_op jit(solution)/shard_map/ppermute | solution.py:27
  726.7 5.9 collective-permute-start.2
  728.6 3.9 copy-start.5
  728.6 15.6 %collective-permute-start.3 = (f32[5,1,6,256]{3,1,2,0:T(1,128)S(1)}, f32[5,1,6,256]{3,1,2,0:T(1,128)S(1)}, u32[]{:S(2)}, u32[]{:S(2)}) collective-permute-start(f32[5,1,6,256]{3,1,2,0:T(1,128)S(1)} %get-tuple-element.17), channel_id=1, source_target_pairs={{0,1},{1,2},{2,3},{3,4},{4,5},{5,6},{6,7},{8,9},{9,10},{10,11},{11... | collective-permute-start | bytes 92168 | tf_op jit(solution)/shard_map/ppermute | solution.py:25
